TPU v7x, 32 devices: a whole 2x2x4 slice. The times are simulated.
32 devices in a mesh: dp: 2 (over core), dom: 16 (over z, y, x).
Axes of the slice: x: 2, y: 2, z: 4, core: 2. Of those that a mesh axis runs over, the one named last changes fastest.
Arguments:
- features: bfloat16 [2, 6144, 512], P('dp', 'dom'), may hold values from -12 to 12
- tile_mask: int32 [2, 48, 18], P('dp', 'dom'), may hold values from 0 to 1, as said below
- cotangent: bfloat16 [2, 6144, 512], P('dp', 'dom'), may hold values from -6 to 6
- w_query: bfloat16 [512, 512], replicated, may hold values from -1 to 1
- w_key: bfloat16 [512, 512], replicated, may hold values from -1 to 1
- w_value: bfloat16 [512, 512], replicated, may hold values from -0.25 to 0.25
- w_out: bfloat16 [512, 512], replicated, may hold values from -0.25 to 0.25
Outputs:
- attended: bfloat16 [2, 6144, 512], P('dp', 'dom')
- grad_features: bfloat16 [2, 6144, 512], P('dp', 'dom')
- grad_query: float32 [512, 512], replicated
- grad_key: float32 [512, 512], replicated
- grad_value: float32 [512, 512], replicated
- grad_out: float32 [512, 512], replicated
Inputs may be any that keep to these rules, and one draw needn't show every extreme that they name: `tile_mask`: 0 or 1; the share of ones differs between tile groups, from about a quarter to all.
All inputs are finite; a program needn't handle non-finite values.
Results may differ from a plain program's by a relative error of at most 0.023.
Values may be sent and summed in bfloat16 or wider, within the bound.
No kernel may reach another device: no remote copies, remote signals or barrier semaphores. Data moves between devices by JAX's collectives and lax.ppermute only.
A program may use at most 128 MiB of HBM per device.

v0:
```python
import jax
import jax.numpy as jnp
from jax import lax
from jax.sharding import PartitionSpec as P

HEADS = 8
HEAD_DIM = 64
TILE = 128
TILE_DEV = 3
NB = 3
CANDT = 18


def with_halo(block, sides, width):
    for axis, dim in sides:
        count = lax.axis_size(axis)
        forward = [(i, i + 1) for i in range(count - 1)]
        forward.append((count - 1, 0))
        backward = [(target, source) for source, target in forward]
        low = lax.ppermute(
            lax.slice_in_dim(block, block.shape[dim] - width, None, axis=dim), axis, forward
        )
        high = lax.ppermute(lax.slice_in_dim(block, 0, width, axis=dim), axis, backward)
        block = jnp.concatenate([low, block, high], axis=dim)
    return block


def from_partner(value, axis, distance):
    mask = 2**distance
    pairs = [(source, source ^ mask) for source in range(lax.axis_size(axis))]
    return lax.ppermute(value, axis, pairs)


def candidate_blocks(block):
    block_rows = block.shape[0]
    near = with_halo(block, (("dom", 0),), block_rows)
    pieces = [block, near[:block_rows], near[2 * block_rows :]]
    levels = lax.axis_size("dom").bit_length() - 1
    for bit_step in range(NB):
        pieces.append(from_partner(block, "dom", levels - 1 - bit_step))
    return pieces


def returned_sum(grad_parts):
    block_rows = grad_parts.shape[1]
    outgoing = jnp.concatenate([grad_parts[1], grad_parts[2]], 0)
    returned = with_halo(outgoing, (("dom", 0),), block_rows)
    summed = grad_parts[0] + returned[:block_rows] + returned[3 * block_rows :]
    levels = lax.axis_size("dom").bit_length() - 1
    for bit_step in range(NB):
        summed = summed + from_partner(grad_parts[3 + bit_step], "dom", levels - 1 - bit_step)
    return summed


def joined(stacked_parts, width_all):
    return jnp.transpose(stacked_parts, (1, 0, 2)).reshape(stacked_parts.shape[1], width_all)


def per_device(features, tile_mask, cotangent, w_query, w_key, w_value, w_out):
    node_rows = features[0]
    block_rows = node_rows.shape[0]
    width_all = node_rows.shape[1]
    highest = lax.Precision.HIGHEST
    factor = HEAD_DIM ** (-0.5)
    w_both = jnp.concatenate([w_key, w_value], 1)
    q_rows = jnp.dot(node_rows, w_query, preferred_element_type=jnp.float32).astype(jnp.bfloat16)
    kv_rows = jnp.dot(node_rows, w_both, preferred_element_type=jnp.float32).astype(jnp.bfloat16)
    pieces = candidate_blocks(node_rows)
    remote = jnp.dot(
        jnp.concatenate(pieces[1:], 0), w_both, preferred_element_type=jnp.float32
    ).astype(jnp.bfloat16)
    cand_kv = jnp.concatenate([kv_rows, remote], 0)
    key_count = cand_kv.shape[0]
    keys_all = cand_kv[:, :width_all]
    values_all = cand_kv[:, width_all:]
    own_tile = jnp.arange(CANDT)[None, :] == jnp.arange(TILE_DEV)[:, None]
    live_tiles = (tile_mask[0] == 1) | own_tile
    masking = jnp.where(live_tiles, 0.0, -1e30).astype(jnp.float32)
    cot_rows = cotangent[0]
    grad_o = jnp.dot(cot_rows, w_out.T, preferred_element_type=jnp.float32).astype(jnp.bfloat16)
    pair_cols = 2 * HEAD_DIM

    def head_pair(pair_index):
        col_start = pair_index * pair_cols
        q_pair = lax.dynamic_slice_in_dim(q_rows, col_start, pair_cols, 1).reshape(
            block_rows, 2, HEAD_DIM
        )
        k_pair = lax.dynamic_slice_in_dim(keys_all, col_start, pair_cols, 1).reshape(
            key_count, 2, HEAD_DIM
        )
        v_pair = lax.dynamic_slice_in_dim(values_all, col_start, pair_cols, 1).reshape(
            key_count, 2, HEAD_DIM
        )
        g_pair = lax.dynamic_slice_in_dim(grad_o, col_start, pair_cols, 1).reshape(
            block_rows, 2, HEAD_DIM
        )
        scores = (
            jnp.einsum("rhd,chd->hrc", q_pair, k_pair, preferred_element_type=jnp.float32) * factor
        )
        scores = scores.reshape(2, TILE_DEV, TILE, CANDT, TILE) + masking[None, :, None, :, None]
        scores = scores.reshape(2, block_rows, key_count)
        row_max = jnp.max(scores, axis=2, keepdims=True)
        exp_vals = jnp.exp(scores - row_max)
        prob_f32 = exp_vals / jnp.sum(exp_vals, axis=2, keepdims=True)
        prob_bf = prob_f32.astype(jnp.bfloat16)
        out_pair = jnp.einsum(
            "hrc,chd->rhd", prob_bf, v_pair, preferred_element_type=jnp.float32
        ).astype(jnp.bfloat16)
        grad_prob = jnp.einsum("rhd,chd->hrc", g_pair, v_pair, preferred_element_type=jnp.float32)
        row_delta = jnp.einsum(
            "rhd,rhd->hr", g_pair.astype(jnp.float32), out_pair.astype(jnp.float32)
        )
        grad_score = (prob_f32 * (grad_prob - row_delta[:, :, None]) * factor).astype(jnp.bfloat16)
        gq_pair = jnp.einsum(
            "hrc,chd->rhd", grad_score, k_pair, preferred_element_type=jnp.float32
        ).reshape(block_rows, pair_cols)
        gk_pair = jnp.einsum(
            "hrc,rhd->chd", grad_score, q_pair, preferred_element_type=jnp.float32
        ).reshape(key_count, pair_cols)
        gv_pair = jnp.einsum(
            "hrc,rhd->chd", prob_bf, g_pair, preferred_element_type=jnp.float32
        ).reshape(key_count, pair_cols)
        return (out_pair.reshape(block_rows, pair_cols), gq_pair, gk_pair, gv_pair)

    stacked = lax.map(head_pair, jnp.arange(HEADS // 2, dtype=jnp.int32))
    out_rows = joined(stacked[0], width_all)
    grad_q = joined(stacked[1], width_all)
    grad_k = joined(stacked[2], width_all)
    grad_v = joined(stacked[3], width_all)
    attended = jnp.dot(out_rows, w_out, preferred_element_type=jnp.float32).astype(jnp.bfloat16)
    grad_parts = jnp.concatenate([grad_k, grad_v], 1).reshape(3 + NB, block_rows, 2 * width_all)
    w_both32 = w_both.astype(jnp.float32)
    rows_f32 = node_rows.astype(jnp.float32)
    contrib = jnp.einsum("scf,df->scd", grad_parts, w_both32, precision=highest)
    kv_dx = returned_sum(contrib)
    cand_rows = (
        jnp.concatenate(pieces, 0).reshape(3 + NB, block_rows, width_all).astype(jnp.float32)
    )
    g_both = jnp.einsum("scd,scf->df", cand_rows, grad_parts, precision=highest)
    grad_x = jnp.dot(grad_q, w_query.astype(jnp.float32).T, precision=highest) + kv_dx
    g_query = jnp.dot(rows_f32.T, grad_q, precision=highest)
    g_out = jnp.dot(out_rows.T, cot_rows, preferred_element_type=jnp.float32)
    g_query, g_key, g_value, g_out = lax.psum(
        (g_query, g_both[:, :width_all], g_both[:, width_all:], g_out), ("dp", "dom")
    )
    return (attended[None], grad_x.astype(jnp.bfloat16)[None], g_query, g_key, g_value, g_out)


def solution(mesh):
    in_specs = (
        P("dp", "dom", None),
        P("dp", "dom", None),
        P("dp", "dom", None),
        P(),
        P(),
        P(),
        P(),
    )
    out_specs = (P("dp", "dom", None), P("dp", "dom", None), P(), P(), P(), P())
    return jax.shard_map(
        per_device, mesh=mesh, in_specs=in_specs, out_specs=out_specs, check_vma=False
    )
```

profile of v0, /device:TPU:0, one launch (start us, length us, event | category | flops | bytes accessed | tf_op | source)
XLA Modules:
  0.0 415.0 jit_solution(7876235823481581899)
XLA Ops:
  7.2 3.1 collective-permute-start.3
  10.4 2.6 collective-permute-start.2
  13.0 2.1 collective-permute-start.1
  16.5 1.8 constant_dynamic-update-slice_fusion.18
  23.2 17.6 %collective-permute-done = bf16[384,512]{1,0:T(8,128)(2,1)} collective-permute-done((bf16[384,512]{1,0:T(8,128)(2,1)}, bf16[384,512]{1,0:T(8,128)(2,1)}, u32[]{:S(2)}, u32[]{:S(2)}) %collective-permute-start) | collective-permute-done | bytes 393248 | tf_op jit(solution)/shard_map/ppermute | solution.py:20
  40.8 1.8 constant_dynamic-update-slice_fusion.17
  42.7 1.8 constant_dynamic-update-slice_fusion.16
  44.5 1.8 constant_dynamic-update-slice_fusion.15
  46.3 1.8 constant_dynamic-update-slice_fusion.14
  48.1 1.8 constant_dynamic-update-slice_fusion.13
  49.9 2.2 convolution_convert_fusion.1
  52.1 3.8 pad_maximum_fusion
  55.9 110.8 %while.16 = (s32[]{:T(128)}, bf16[4,384,128]{1,2,0:T(8,128)(2,1)}, f32[4,384,128]{1,2,0:T(8,128)}, f32[4,2304,128]{1,2,0:T(8,128)}, f32[4,2304,128]{1,2,0:T(8,12...) while((s32[]{:T(128)}, bf16[4,384,128]{1,2,0:T(8,128)(2,1)}, ...), condition=%wide.region_3.4_spmd, body=%wide.region_0.3_spmd.sunk | while | flops 1378665984 | bytes 104414744 | solution.py:125
  60.7 2.5 copy.52
  63.2 7.1 %fusion.91 = (f32[2,384]{1,0:T(2,128)S(1)}, f32[2,384,2304]{2,1,0:T(8,128)}) fusion(f32[384,2304]{1,0:T(8,128)} %bitcast.170, bf16[384,2,64]{0,2,1:T(8,128)(2,1)S(1)} %bitcast.177, bf16[2304,2,64]{0,2,1:T(8,128)(2,1)S(1)} %bitcast.171), kind=kOutput, calls=%fused_computation.77.clone.1 | convolution fusion | flops 233572608 | bytes 11308032 | tf_op jit(solution)/shard_map/while/body/eval_jaxpr/sub | solution.py:103
  70.3 3.8 fusion.92
  77.1 1.6 multiply_convert_fusion.2
  82.0 1.7 constant_dynamic-update-slice_fusion.24
  88.4 2.5 copy.52
  90.9 7.1 %fusion.91 = (f32[2,384]{1,0:T(2,128)S(1)}, f32[2,384,2304]{2,1,0:T(8,128)}) fusion(f32[384,2304]{1,0:T(8,128)} %bitcast.170, bf16[384,2,64]{0,2,1:T(8,128)(2,1)S(1)} %bitcast.177, bf16[2304,2,64]{0,2,1:T(8,128)(2,1)S(1)} %bitcast.171), kind=kOutput, calls=%fused_computation.77.clone.1 | convolution fusion | flops 233572608 | bytes 11308032 | tf_op jit(solution)/shard_map/while/body/eval_jaxpr/sub | solution.py:103
  98.0 3.8 fusion.92
  104.9 1.6 multiply_convert_fusion.2
  109.8 1.6 constant_dynamic-update-slice_fusion.24
  116.2 2.5 copy.52
  118.7 7.1 %fusion.91 = (f32[2,384]{1,0:T(2,128)S(1)}, f32[2,384,2304]{2,1,0:T(8,128)}) fusion(f32[384,2304]{1,0:T(8,128)} %bitcast.170, bf16[384,2,64]{0,2,1:T(8,128)(2,1)S(1)} %bitcast.177, bf16[2304,2,64]{0,2,1:T(8,128)(2,1)S(1)} %bitcast.171), kind=kOutput, calls=%fused_computation.77.clone.1 | convolution fusion | flops 233572608 | bytes 11308032 | tf_op jit(solution)/shard_map/while/body/eval_jaxpr/sub | solution.py:103
  125.8 3.8 fusion.92
  132.6 1.6 multiply_convert_fusion.2
  143.8 2.5 copy.52
  146.3 7.1 %fusion.91 = (f32[2,384]{1,0:T(2,128)S(1)}, f32[2,384,2304]{2,1,0:T(8,128)}) fusion(f32[384,2304]{1,0:T(8,128)} %bitcast.170, bf16[384,2,64]{0,2,1:T(8,128)(2,1)S(1)} %bitcast.177, bf16[2304,2,64]{0,2,1:T(8,128)(2,1)S(1)} %bitcast.171), kind=kOutput, calls=%fused_computation.77.clone.1 | convolution fusion | flops 233572608 | bytes 11308032 | tf_op jit(solution)/shard_map/while/body/eval_jaxpr/sub | solution.py:103
  153.4 3.8 fusion.92
  160.3 1.6 multiply_convert_fusion.2
  166.7 6.4 %copy.25 = f32[2304,4,128]{2,1,0:T(4,128)} copy(f32[2304,4,128]{0,2,1:T(8,128)} %bitcast.185) | data formatting | bytes 9437184 | tf_op jit(solution)/shard_map/transpose | solution.py:56
  173.2 6.7 %concatenate.24 = f32[6,384,512]{2,1,0:T(8,128)} reshape(f32[2304,4,128]{2,1,0:T(4,128)} %copy.25) | data formatting | bytes 9437184 | tf_op jit(solution)/shard_map/concatenate | solution.py:131
  181.3 2.0 convolution_bitcast_fusion.1
  183.2 6.5 %copy.24 = f32[2304,4,128]{2,1,0:T(4,128)} copy(f32[2304,4,128]{0,2,1:T(8,128)} %bitcast.186) | data formatting | bytes 9437184 | tf_op jit(solution)/shard_map/transpose | solution.py:56
  189.7 6.6 %concatenate.23 = f32[6,384,512]{2,1,0:T(8,128)} reshape(f32[2304,4,128]{2,1,0:T(4,128)} %copy.24) | data formatting | bytes 9437184 | tf_op jit(solution)/shard_map/concatenate | solution.py:131
  196.3 3.0 constant_dynamic-update-slice_fusion.12
  202.0 7.7 %convolution_bitcast_fusion = f32[512,1024]{1,0:T(8,128)S(1)} fusion(bf16[6,384,512]{2,1,0:T(8,128)(2,1)S(1)} %bitcast.196, f32[6,384,1024]{2,1,0:T(8,128)S(1)} %constant_dynamic-update-slice_fusion.11), kind=kOutput, calls=%fused_computation.28 | convolution fusion | flops 14495514624 | bytes 13893632 | tf_op jit(solution)/shard_map/scd,scf->df/dot_general | solution.py:139
  211.2 10.5 %fusion.12 = f32[6,384,512]{2,1,0:T(8,128)S(1)} fusion(f32[6,384,1024]{2,1,0:T(8,128)} %copy-done.4, bf16[512,1024]{1,0:T(8,128)(2,1)S(1)} %copy-done.15), kind=kOutput, calls=%fused_computation.36 | convolution fusion | flops 14495514624 | bytes 15204352 | tf_op jit(solution)/shard_map/scf,df->scd/dot_general | solution.py:134
  224.4 4.2 %collective-permute-start.6 = (f32[384,512]{1,0:T(8,128)S(1)}, f32[384,512]{1,0:T(8,128)S(1)}, u32[]{:S(2)}, u32[]{:S(2)}) collective-permute-start(f32[384,512]{1,0:T(8,128)S(1)} %get-tuple-element.140), channel_id=1, source_target_pairs={{1,0},{2,1},{3,2},{4,3},{5,4},{6,5},{7,6},{8,7},{9,8},{10,9},{11,1... | collective-permute-start | bytes 2359304 | tf_op jit(solution)/shard_map/ppermute | solution.py:23
  229.8 24.6 %collective-permute-done.5 = f32[384,512]{1,0:T(8,128)S(1)} collective-permute-done((f32[384,512]{1,0:T(8,128)S(1)}, f32[384,512]{1,0:T(8,128)S(1)}, u32[]{:S(2)}, u32[]{:S(2)}) %collective-permute-start.5) | collective-permute-done | bytes 786464 | tf_op jit(solution)/shard_map/ppermute | solution.py:20
  254.4 7.0 %collective-permute-done.9 = f32[384,512]{1,0:T(8,128)S(1)} collective-permute-done((f32[384,512]{1,0:T(8,128)S(1)}, f32[384,512]{1,0:T(8,128)S(1)}, u32[]{:S(2)}, u32[]{:S(2)}) %collective-permute-start.9) | collective-permute-done | bytes 786464 | tf_op jit(solution)/shard_map/ppermute | solution.py:31
  261.4 9.6 %collective-permute-done.8 = f32[384,512]{1,0:T(8,128)S(1)} collective-permute-done((f32[384,512]{1,0:T(8,128)S(1)}, f32[384,512]{1,0:T(8,128)S(1)}, u32[]{:S(2)}, u32[]{:S(2)}) %collective-permute-start.8) | collective-permute-done | bytes 786464 | tf_op jit(solution)/shard_map/ppermute | solution.py:31
  271.4 16.0 %collective-permute-done.6 = f32[384,512]{1,0:T(8,128)S(1)} collective-permute-done((f32[384,512]{1,0:T(8,128)S(1)}, f32[384,512]{1,0:T(8,128)S(1)}, u32[]{:S(2)}, u32[]{:S(2)}) %collective-permute-start.6) | collective-permute-done | bytes 786464 | tf_op jit(solution)/shard_map/ppermute | solution.py:23
  287.4 2.4 fusion.21
  289.8 111.5 %all-reduce.3.cloned.1.call-done = (f32[512,512]{0,1:T(8,128)}, f32[512,512]{1,0:T(8,128)}, f32[512,512]{1,0:T(8,128)}, f32[512,512]{1,0:T(8,128)}) async-done(((f32[512,512]{0,1:T(8,128)}, f32[512,512]{1,0:T(8,128)}, f32[512,512]{1,0:T(8,128)}, f32[512,512]{1,0:T(8,128)}), (f32[512,512]{0,1:T(8,128)}, f32[512,512]{1,0:T(8,128)}, f32[512,512]{1,0:T(8,128)}, ...) | async-done | bytes 4194320 | tf_op jit(solution)/shard_map/psum | solution.py:143
  401.2 2.7 copy.27
  403.9 2.3 copy.89
  (157 shorter events, 62.2 us)
Async XLA Ops:
  7.2 15.5 %copy-start = (bf16[512,512]{1,0:T(8,128)(2,1)S(1)}, bf16[512,512]{1,0:T(8,128)(2,1)}, u32[]{:S(2)}) copy-start(bf16[512,512]{1,0:T(8,128)(2,1)} %param.15) | copy-start | bytes 1572868
  7.2 14.9 %copy-start.2 = (bf16[1,384,512]{2,1,0:T(8,128)(2,1)S(1)}, bf16[1,384,512]{2,1,0:T(8,128)(2,1)}, u32[]{:S(2)}) copy-start(bf16[1,384,512]{2,1,0:T(8,128)(2,1)} %param.9) | copy-start | bytes 1179652
  7.2 15.5 %copy-start.8 = (bf16[1,384,512]{2,1,0:T(8,128)(2,1)S(1)}, bf16[1,384,512]{2,1,0:T(8,128)(2,1)}, u32[]{:S(2)}) copy-start(bf16[1,384,512]{2,1,0:T(8,128)(2,1)} %param.11) | copy-start | bytes 1179652
  7.2 394.0 %all-reduce.3.cloned.1.call-start = ((), (), s32[]{:S(2)}) async-start(), calls=%async_computation | async-start | bytes 8388608 | tf_op jit(solution)/shard_map/psum | solution.py:143
  7.2 39.0 %collective-permute-start.3 = (bf16[384,512]{1,0:T(8,128)(2,1)}, bf16[384,512]{1,0:T(8,128)(2,1)}, u32[]{:S(2)}, u32[]{:S(2)}) collective-permute-start(bf16[384,512]{1,0:T(8,128)(2,1)} %bitcast.187), channel_id=1, source_target_pairs={{0,4},{1,5},{2,6},{3,7},{4,0},{5,1},{6,2},{7,3},{8,12},{9,13},{10,... | collective-permute-start | bytes 1179656 | tf_op jit(solution)/shard_map/ppermute | solution.py:31
  10.4 34.1 %collective-permute-start.2 = (bf16[384,512]{1,0:T(8,128)(2,1)}, bf16[384,512]{1,0:T(8,128)(2,1)}, u32[]{:S(2)}, u32[]{:S(2)}) collective-permute-start(bf16[384,512]{1,0:T(8,128)(2,1)} %bitcast.188), channel_id=1, source_target_pairs={{0,8},{1,9},{2,10},{3,11},{4,12},{5,13},{6,14},{7,15},{8,0},{9,1},... | collective-permute-start | bytes 1179656 | tf_op jit(solution)/shard_map/ppermute | solution.py:31
  13.0 29.7 %collective-permute-start.1 = (bf16[384,512]{1,0:T(8,128)(2,1)}, bf16[384,512]{1,0:T(8,128)(2,1)}, u32[]{:S(2)}, u32[]{:S(2)}) collective-permute-start(bf16[384,512]{1,0:T(8,128)(2,1)} %bitcast.189), channel_id=1, source_target_pairs={{1,0},{2,1},{3,2},{4,3},{5,4},{6,5},{7,6},{8,7},{9,8},{10,9},{11,1... | collective-permute-start | bytes 1179656 | tf_op jit(solution)/shard_map/ppermute | solution.py:23
  15.1 25.8 %collective-permute-start = (bf16[384,512]{1,0:T(8,128)(2,1)}, bf16[384,512]{1,0:T(8,128)(2,1)}, u32[]{:S(2)}, u32[]{:S(2)}) collective-permute-start(bf16[384,512]{1,0:T(8,128)(2,1)} %bitcast.190), channel_id=1, source_target_pairs={{0,1},{1,2},{2,3},{3,4},{4,5},{5,6},{6,7},{7,8},{8,9},{9,10},{10,1... | collective-permute-start | bytes 1179656 | tf_op jit(solution)/shard_map/ppermute | solution.py:20
  15.1 33.0 %collective-permute-start.4 = (bf16[384,512]{1,0:T(8,128)(2,1)}, bf16[384,512]{1,0:T(8,128)(2,1)}, u32[]{:S(2)}, u32[]{:S(2)}) collective-permute-start(bf16[384,512]{1,0:T(8,128)(2,1)} %bitcast.191), channel_id=1, source_target_pairs={{0,2},{1,3},{2,0},{3,1},{4,6},{5,7},{6,4},{7,5},{8,10},{9,11},{10,... | collective-permute-start | bytes 1179656 | tf_op jit(solution)/shard_map/ppermute | solution.py:31
  18.3 4.8 %copy-start.17 = (s32[1,3,18]{2,0,1:T(1,128)S(1)}, s32[1,3,18]{2,0,1:T(1,128)}, u32[]{:S(2)}) copy-start(s32[1,3,18]{2,0,1:T(1,128)} %param.10) | copy-start | bytes 652
  22.1 1.0 copy-start.13
  23.2 26.7 %copy-start.14 = (bf16[512,1024]{1,0:T(8,128)(2,1)S(1)}, bf16[512,1024]{1,0:T(8,128)(2,1)}, u32[]{:S(2)}) copy-start(bf16[512,1024]{1,0:T(8,128)(2,1)} %copy-done.13) | copy-start | bytes 3145732
  55.9 1.5 copy-start.6
  74.1 3.0 copy-start.1
  80.7 3.0 copy-start.7
  83.7 1.5 copy-start.6
  101.9 3.0 copy-start.1
  108.5 3.0 copy-start.7
  111.4 1.5 copy-start.6
  129.6 3.0 copy-start.1
  136.2 2.9 copy-start.7
  139.1 1.5 copy-start.6
  157.2 3.0 copy-start.1
  163.8 2.9 copy-start.7
  173.2 6.7 %copy-start.9 = (bf16[1,384,512]{2,1,0:T(8,128)(2,1)S(1)}, bf16[1,384,512]{2,1,0:T(8,128)(2,1)}, u32[]{:S(2)}) copy-start(bf16[1,384,512]{2,1,0:T(8,128)(2,1)} %param.11) | copy-start | bytes 1179652
  173.2 6.7 %copy-start.10 = (bf16[4,384,128]{1,2,0:T(8,128)(2,1)S(1)}, bf16[4,384,128]{1,2,0:T(8,128)(2,1)}, u32[]{:S(2)}) copy-start(bf16[4,384,128]{1,2,0:T(8,128)(2,1)} %get-tuple-element.66) | copy-start | bytes 1179652
  173.2 8.1 %copy-start.3 = (f32[4,384,128]{1,2,0:T(8,128)S(1)}, f32[4,384,128]{1,2,0:T(8,128)}, u32[]{:S(2)}) copy-start(f32[4,384,128]{1,2,0:T(8,128)} %get-tuple-element.67) | copy-start | bytes 2359300
  189.7 9.6 %slice-start = ((s8[4718592]{0:T(1024)(128)(4,1)}), s8[524288]{0:T(1024)(128)(4,1)S(1)}, s32[]{:S(2)}) async-start(s8[4718592]{0:T(1024)(128)(4,1)} %bitcast.182), calls=%async_computation.1 | async-start | bytes 1048576
  196.3 3.6 slice-start.1
  199.9 2.1 copy-start.16
  200.4 9.3 %copy-start.4 = (f32[6,384,1024]{2,1,0:T(8,128)}, f32[6,384,1024]{2,1,0:T(8,128)S(1)}, u32[]{:S(2)}) copy-start(f32[6,384,1024]{2,1,0:T(8,128)S(1)} %constant_dynamic-update-slice_fusion.11) | copy-start | bytes 28311556
  209.7 1.5 copy-start.15
  221.7 65.7 %copy-start.5 = (bf16[512,512]{1,0:T(8,128)(2,1)S(1)}, bf16[512,512]{1,0:T(8,128)(2,1)}, u32[]{:S(2)}) copy-start(bf16[512,512]{1,0:T(8,128)(2,1)} %param.12) | copy-start | bytes 1572868
  222.2 32.2 %collective-permute-start.5 = (f32[384,512]{1,0:T(8,128)S(1)}, f32[384,512]{1,0:T(8,128)S(1)}, u32[]{:S(2)}, u32[]{:S(2)}) collective-permute-start(f32[384,512]{1,0:T(8,128)S(1)} %get-tuple-element.136), channel_id=1, source_target_pairs={{0,1},{1,2},{2,3},{3,4},{4,5},{5,6},{6,7},{7,8},{8,9},{9,10},{10,1... | collective-permute-start | bytes 2359304 | tf_op jit(solution)/shard_map/ppermute | solution.py:20
  222.2 39.2 %collective-permute-start.9 = (f32[384,512]{1,0:T(8,128)S(1)}, f32[384,512]{1,0:T(8,128)S(1)}, u32[]{:S(2)}, u32[]{:S(2)}) collective-permute-start(f32[384,512]{1,0:T(8,128)S(1)} %get-tuple-element.137), channel_id=1, source_target_pairs={{0,2},{1,3},{2,0},{3,1},{4,6},{5,7},{6,4},{7,5},{8,10},{9,11},{10,... | collective-permute-start | bytes 2359304 | tf_op jit(solution)/shard_map/ppermute | solution.py:31
  222.3 48.7 %collective-permute-start.8 = (f32[384,512]{1,0:T(8,128)S(1)}, f32[384,512]{1,0:T(8,128)S(1)}, u32[]{:S(2)}, u32[]{:S(2)}) collective-permute-start(f32[384,512]{1,0:T(8,128)S(1)} %get-tuple-element.138), channel_id=1, source_target_pairs={{0,4},{1,5},{2,6},{3,7},{4,0},{5,1},{6,2},{7,3},{8,12},{9,13},{10,... | collective-permute-start | bytes 2359304 | tf_op jit(solution)/shard_map/ppermute | solution.py:31
  223.1 48.3 %collective-permute-start.7 = (f32[384,512]{1,0:T(8,128)S(1)}, f32[384,512]{1,0:T(8,128)S(1)}, u32[]{:S(2)}, u32[]{:S(2)}) collective-permute-start(f32[384,512]{1,0:T(8,128)S(1)} %get-tuple-element.139), channel_id=1, source_target_pairs={{0,8},{1,9},{2,10},{3,11},{4,12},{5,13},{6,14},{7,15},{8,0},{9,1},... | collective-permute-start | bytes 2359304 | tf_op jit(solution)/shard_map/ppermute | solution.py:31
  224.4 63.0 %collective-permute-start.6 = (f32[384,512]{1,0:T(8,128)S(1)}, f32[384,512]{1,0:T(8,128)S(1)}, u32[]{:S(2)}, u32[]{:S(2)}) collective-permute-start(f32[384,512]{1,0:T(8,128)S(1)} %get-tuple-element.140), channel_id=1, source_target_pairs={{1,0},{2,1},{3,2},{4,3},{5,4},{6,5},{7,6},{8,7},{9,8},{10,9},{11,1... | collective-permute-start | bytes 2359304 | tf_op jit(solution)/shard_map/ppermute | solution.py:23
  401.2 4.9 %copy-start.12 = (f32[512,512]{1,0:T(8,128)S(1)}, f32[512,512]{1,0:T(8,128)}, u32[]{:S(2)}) copy-start(f32[512,512]{1,0:T(8,128)} %get-tuple-element.283) | copy-start | bytes 3145732
  401.2 5.9 %copy-start.11 = (f32[512,512]{1,0:T(8,128)S(1)}, f32[512,512]{1,0:T(8,128)}, u32[]{:S(2)}) copy-start(f32[512,512]{1,0:T(8,128)} %get-tuple-element.284) | copy-start | bytes 3145732
Sparse Core Ops, SparseCore 0:
  211.3 189.8 all-reduce.2
where the time goes:
time: 417 us; the launch traced here: 415 us
  waiting for transfers between devices  187 us (45%)
  local copies, waits for them, and re-layouts  95.9 us (23%)
  matrix products  80.1 us (19%)
  other arithmetic  19.1 us (5%)
  starting transfers between devices  15.7 us (4%)
  between operations  14.3 us (3%)
    psum x1, waiting for transfers between devices, per_device(): lax.psum((g_query, g_both[:, :width_all], g_both[:, width_all:], g_out),...  111 us
    ppermute x2, waiting for transfers between devices, with_halo(): lax.ppermute(lax.slice_in_dim(block, block.shape[dim] - width, None, axis...  42.2 us
    sub x4, matrix products, head_pair(): exp_vals = jnp.exp(scores - row_max)  28.4 us
    unnamed x45, local copies, waits for them, and re-layouts  22.3 us
    ppermute x6, waiting for transfers between devices, from_partner(): return lax.ppermute(value, axis, pairs)  17 us
    ppermute x2, waiting for transfers between devices, with_halo(): lax.ppermute(lax.slice_in_dim(block, 0, width, axis=dim), axis, backward)  16 us
    convert_element_type x4, other arithmetic, head_pair(): prob_bf = prob_f32.astype(jnp.bfloat16)  15.3 us
    while x28, local copies, waits for them, and re-layouts  14.3 us
  transfers between devices with their start and end apart: 11, of which 7 were waited for; matrix products, arithmetic and copies ran while one was open for 7% of the time, Pallas kernels for 0%

commit v1 on v0

v1 whole, which is shorter than its diff:
```python
import jax
import jax.numpy as jnp
from jax import lax
from jax.experimental import pallas as pl
from jax.experimental.pallas import tpu as pltpu
from jax.sharding import PartitionSpec as P

HEAD_DIM = 64
TILE = 128
NB = 3
LANES = 128
NT = (((1,), (1,)), ((), ()))
NN = (((1,), (0,)), ((), ()))
TN = (((0,), (0,)), ((), ()))
F32 = jnp.float32
BF = jnp.bfloat16


def exchanged(value, axis, mask):
    pairs = [(source, source ^ mask) for source in range(lax.axis_size(axis))]
    return lax.ppermute(value, axis, pairs)


def shifted(value, axis, step):
    count = lax.axis_size(axis)
    return lax.ppermute(value, axis, [(i, (i + step) % count) for i in range(count)])


def attention_kernel(
    q_ref, k_ref, v_ref, go_ref, bias_ref, o_ref, gq_ref, gk_ref, gv_ref,
    k_aug, v_aug, exp_all, score_all, q_all, go_all,
):
    rows = q_ref.shape[0]
    keys = k_ref.shape[0]
    lane = lax.broadcasted_iota(jnp.int32, (rows, LANES), 1)
    row = lax.broadcasted_iota(jnp.int32, (rows, LANES), 0)
    k_aug[:, :LANES] = k_ref[...]
    k_aug[:, LANES:] = bias_ref[...]
    v_aug[:, :LANES] = v_ref[...]
    v_aug[:, LANES:] = jnp.ones((keys, LANES), BF)
    one_hot = (row // TILE == lane).astype(F32).astype(BF)
    factor = HEAD_DIM**-0.5
    q_pair = q_ref[...].astype(F32) * factor
    go_pair = go_ref[...].astype(F32)
    outs = []
    grads = []
    for head in range(2):
        mine = (lane < HEAD_DIM) if head == 0 else (lane >= HEAD_DIM)
        span = pl.ds(head * rows, rows)
        q_head = jnp.where(mine, q_pair, 0.0).astype(BF)
        q_all[span, :] = q_head
        scores = lax.dot_general(
            jnp.concatenate([q_head, one_hot], 1), k_aug[...], NT, preferred_element_type=F32
        )
        row_max = jnp.max(scores, axis=1, keepdims=True)
        exp_vals = jnp.exp(scores - row_max).astype(BF)
        exp_all[span, :] = exp_vals
        summed = lax.dot_general(exp_vals, v_aug[...], NN, preferred_element_type=F32)
        inverse = 1.0 / summed[:, LANES:]
        out = (summed[:, :LANES] * inverse).astype(BF)
        outs.append(out)
        go_head = jnp.where(mine, go_pair * inverse, 0.0).astype(BF)
        go_all[span, :] = go_head
        delta = jnp.sum(go_head.astype(F32) * out.astype(F32), axis=1, keepdims=True)
        high = delta.astype(BF).astype(F32)
        low = delta - high
        less = jnp.where(lane == 0, -high, jnp.where(lane == 1, -low, 0.0)).astype(BF)
        grad_prob = lax.dot_general(
            jnp.concatenate([go_head, less], 1), v_aug[...], NT, preferred_element_type=F32
        )
        grad_score = grad_prob.astype(BF) * exp_vals
        score_all[span, :] = grad_score
        grads.append(
            lax.dot_general(grad_score, k_aug[:, :LANES], NN, preferred_element_type=F32) * factor
        )
    first = lane < HEAD_DIM
    o_ref[...] = jnp.where(first, outs[0].astype(F32), outs[1].astype(F32)).astype(BF)
    gq_ref[...] = jnp.where(first, grads[0], grads[1]).astype(BF)
    gv_ref[...] = lax.dot_general(
        go_all[...].T, exp_all[...], NN, preferred_element_type=F32
    ).astype(BF)
    gk_ref[...] = lax.dot_general(
        q_all[...].T, score_all[...], NN, preferred_element_type=F32
    ).astype(BF)


def attention(q, k, v, go, bias):
    rows, width = q.shape
    keys = k.shape[0]
    by_rows = pl.BlockSpec((rows, LANES), lambda pair: (0, pair))
    by_keys = pl.BlockSpec((keys, LANES), lambda pair: (0, pair))
    turned = pl.BlockSpec((LANES, keys), lambda pair: (pair, 0))
    return pl.pallas_call(
        attention_kernel,
        grid=(width // LANES,),
        in_specs=[
            by_rows, by_keys, by_keys, by_rows, pl.BlockSpec((keys, LANES), lambda pair: (0, 0)),
        ],
        out_specs=[by_rows, by_rows, turned, turned],
        out_shape=[
            jax.ShapeDtypeStruct((rows, width), BF),
            jax.ShapeDtypeStruct((rows, width), BF),
            jax.ShapeDtypeStruct((width, keys), BF),
            jax.ShapeDtypeStruct((width, keys), BF),
        ],
        scratch_shapes=[
            pltpu.VMEM((keys, 2 * LANES), BF),
            pltpu.VMEM((keys, 2 * LANES), BF),
            pltpu.VMEM((2 * rows, keys), BF),
            pltpu.VMEM((2 * rows, keys), BF),
            pltpu.VMEM((2 * rows, LANES), BF),
            pltpu.VMEM((2 * rows, LANES), BF),
        ],
        compiler_params=pltpu.CompilerParams(vmem_limit_bytes=60 * 1024 * 1024),
        name="attention",
    )(q, k, v, go, bias)


def sum_stages():
    stages = [("dp", (1,), 0)]
    bits = lax.axis_size("dom").bit_length() - 1
    bit = 0
    while bit < bits:
        width = min(2, bits - bit)
        stages.append(("dom", tuple(m << bit for m in range(1, 1 << width)), bit))
        bit += width
    return stages


def chunk_of(value, index, count):
    size = value.shape[0] // count
    return lax.dynamic_slice_in_dim(value, index * size, size, 0)


def summed_over_devices(value):
    stages = sum_stages()
    for axis, masks, bit in stages:
        count = len(masks) + 1
        mine = (lax.axis_index(axis) >> bit) % count
        total = chunk_of(value, mine, count).astype(F32)
        for mask in masks:
            sent = chunk_of(value, mine ^ (mask >> bit), count)
            total = total + exchanged(sent, axis, mask).astype(F32)
        value = total.astype(BF)
    for axis, masks, bit in reversed(stages):
        count = len(masks) + 1
        mine = (lax.axis_index(axis) >> bit) % count
        size = value.shape[0]
        whole = jnp.zeros((count * size,) + value.shape[1:], BF)
        whole = lax.dynamic_update_slice_in_dim(whole, value, mine * size, 0)
        for mask in masks:
            got = exchanged(value, axis, mask)
            whole = lax.dynamic_update_slice_in_dim(whole, got, (mine ^ (mask >> bit)) * size, 0)
        value = whole
    return value


def per_device(features, tile_mask, cotangent, w_query, w_key, w_value, w_out):
    x = features[0]
    rows, width = x.shape
    cot = cotangent[0]
    levels = lax.axis_size("dom").bit_length() - 1
    steps = [1 << (levels - 1 - j) for j in range(NB)]
    far = [exchanged(x, "dom", step) for step in steps]
    below = shifted(x, "dom", 1)
    above = shifted(x, "dom", -1)
    w_both = jnp.concatenate([w_key, w_value], 1)
    q = jnp.dot(x, w_query, preferred_element_type=F32).astype(BF)
    go = lax.dot_general(cot, w_out, NT, preferred_element_type=F32).astype(BF)
    tiles, cands = tile_mask.shape[1:]
    own = jnp.arange(cands)[None, :] == jnp.arange(tiles)[:, None]
    live = (tile_mask[0] == 1) | own
    bias = jnp.pad(jnp.where(live, 0.0, -1e30).T, ((0, 0), (0, LANES - tiles)))
    bias = jnp.repeat(bias.astype(BF), TILE, axis=0)
    cand = jnp.concatenate([x, below, above] + far, 0)
    k = jnp.dot(cand, w_key, preferred_element_type=F32).astype(BF)
    v = jnp.dot(cand, w_value, preferred_element_type=F32).astype(BF)
    o, gq, gk, gv = attention(q, k, v, go, bias)
    attended = jnp.dot(o, w_out, preferred_element_type=F32).astype(BF)
    contrib = lax.dot_general(gk, w_key, (((0,), (1,)), ((), ())), preferred_element_type=F32)
    contrib = contrib + lax.dot_general(
        gv, w_value, (((0,), (1,)), ((), ())), preferred_element_type=F32
    )
    parts = contrib.reshape(3 + NB, rows, width)
    sent = parts.astype(BF)
    back = [exchanged(sent[3 + j], "dom", steps[j]) for j in range(NB)]
    back.append(shifted(sent[1], "dom", -1))
    back.append(shifted(sent[2], "dom", 1))
    grad_x = parts[0] + lax.dot_general(gq, w_query, NT, preferred_element_type=F32)
    g_query = lax.dot_general(x, gq, TN, preferred_element_type=F32)
    g_key = lax.dot_general(cand, gk, (((0,), (1,)), ((), ())), preferred_element_type=F32)
    g_value = lax.dot_general(cand, gv, (((0,), (1,)), ((), ())), preferred_element_type=F32)
    g_out = lax.dot_general(o, cot, TN, preferred_element_type=F32)
    grads = jnp.concatenate([g.astype(BF) for g in (g_query, g_key, g_value, g_out)], 0)
    grads = summed_over_devices(grads).astype(F32)
    for part in back:
        grad_x = grad_x + part.astype(F32)
    g_query, g_key, g_value, g_out = jnp.split(grads, 4, 0)
    return (attended[None], grad_x.astype(BF)[None], g_query, g_key, g_value, g_out)


def solution(mesh):
    split = P("dp", "dom", None)
    return jax.shard_map(
        per_device,
        mesh=mesh,
        in_specs=(split, split, split, P(), P(), P(), P()),
        out_specs=(split, split, P(), P(), P(), P()),
        check_vma=False,
    )
```

time: 417 us -> 164 us (0.39)
  waiting for transfers between devices: 187 us -> 59 us
  local copies, waits for them, and re-layouts: 95.9 us -> 12.6 us
  matrix products: 80.1 us -> 24.2 us
  Pallas kernels: 0 us -> 31.6 us
  starting transfers between devices: 15.7 us -> 32.6 us
  other arithmetic: 19.1 us -> 2.95 us
  between operations: 14.3 us -> 0.99 us
    psum x1 -> x0, waiting for transfers between devices: 111 us -> none  [per_device(): lax.psum((g_query, g_both[:, :width_all], g_both[:, width_all:], g_out),...]
    pallas_call x0 -> x1, Pallas kernels: none -> 31.6 us  [attention(): pl.pallas_call(attention_kernel, grid=(width // LANES,), in_specs=[by_row...]
    sub x4 -> x0, matrix products: 28.4 us -> none  [head_pair(): exp_vals = jnp.exp(scores - row_max)]
    dot_general x30 -> x12, matrix products: 51.7 us -> 24.2 us  [the longest x1 4.62 us: per_device(): v = jnp.dot(cand, w_value, preferred_element_type=F32).astype(BF)]
    ppermute x10 -> x24, starting transfers between devices: 15.7 us -> 32.6 us  [the longest x20 22.6 us: exchanged(): return lax.ppermute(value, axis, pairs)]
    unnamed x45 -> x36, local copies, waits for them, and re-layouts: 22.3 us -> 6.06 us
    ppermute x10 -> x24, waiting for transfers between devices: 75.2 us -> 59 us  [the longest x20 45.8 us: exchanged(): return lax.ppermute(value, axis, pairs)]
    concatenate x5 -> x1, local copies, waits for them, and re-layouts: 16.7 us -> 0.78 us  [per_device(): cand = jnp.concatenate([x, below, above] + far, 0)]
  transfers between devices with their start and end apart: 11 -> 24, of which waited for: 7 -> 16; matrix products, arithmetic and copies ran while one was open for 7% -> 10% of each run, Pallas kernels for 0% -> 0%
where the time goes in v1:
time: 164 us
  waiting for transfers between devices  59 us (36%)
  starting transfers between devices  32.6 us (20%)
  Pallas kernels  31.6 us (19%)
  matrix products  24.2 us (15%)
  local copies, waits for them, and re-layouts  12.6 us (8%)
  other arithmetic  2.95 us (2%)
    ppermute x20, waiting for transfers between devices, exchanged(): return lax.ppermute(value, axis, pairs)  45.8 us
    pallas_call x1, Pallas kernels, attention(): pl.pallas_call(attention_kernel, grid=(width // LANES,), in_specs=[by_row...  31.6 us
    ppermute x20, starting transfers between devices, exchanged(): return lax.ppermute(value, axis, pairs)  22.6 us
    ppermute x4, waiting for transfers between devices, shifted(): lax.ppermute(value, axis, [(i, (i + step) % count) for i in range(count)])  13.2 us
    ppermute x4, starting transfers between devices, shifted(): lax.ppermute(value, axis, [(i, (i + step) % count) for i in range(count)])  10 us
    unnamed x36, local copies, waits for them, and re-layouts  6.06 us
    dot_general x1, matrix products, per_device(): v = jnp.dot(cand, w_value, preferred_element_type=F32).astype(BF)  4.62 us
  transfers between devices with their start and end apart: 24, of which 16 were waited for; matrix products, arithmetic and copies ran while one was open for 10% of the time, Pallas kernels for 0%

profile of v1, /device:TPU:0, one launch (start us, length us, event | category | flops | bytes accessed | tf_op | source)
XLA Modules:
  0.0 164.0 jit_solution(8937049633478258267)
XLA Ops:
  0.7 3.0 %collective-permute-start = (bf16[384,512]{1,0:T(8,128)(2,1)}, bf16[384,512]{1,0:T(8,128)(2,1)S(1)}, u32[]{:S(2)}, u32[]{:S(2)}) collective-permute-start(bf16[384,512]{1,0:T(8,128)(2,1)} %bitcast.44), channel_id=1, source_target_pairs={{0,1},{1,2},{2,3},{3,4},{4,5},{5,6},{6,7},{7,8},{8,9},{9,10},{10,1... | collective-permute-start | bytes 1179656 | tf_op jit(solution)/shard_map/ppermute | solution.py:26
  3.7 4.1 %collective-permute-start.1 = (bf16[384,512]{1,0:T(8,128)(2,1)}, bf16[384,512]{1,0:T(8,128)(2,1)S(1)}, u32[]{:S(2)}, u32[]{:S(2)}) collective-permute-start(bf16[384,512]{1,0:T(8,128)(2,1)} %bitcast.45), channel_id=1, source_target_pairs={{0,15},{1,0},{2,1},{3,2},{4,3},{5,4},{6,5},{7,6},{8,7},{9,8},{10,9... | collective-permute-start | bytes 1179656 | tf_op jit(solution)/shard_map/ppermute | solution.py:26
  7.7 0.9 collective-permute-start.2
  8.6 1.6 collective-permute-start.3
  10.8 1.8 %constant_dynamic-update-slice_fusion.5 = bf16[2304,512]{1,0:T(8,128)(2,1)} fusion(bf16[1,384,512]{2,1,0:T(8,128)(2,1)} %param.7), kind=kLoop, calls=%fused_computation.26 | loop fusion | bytes 786432
  12.6 2.3 %convolution_convert_fusion.8.q_ref = bf16[384,512]{1,0:T(8,128)(2,1)} fusion(bf16[512,512]{1,0:T(8,128)(2,1)} %param.10, bf16[1,384,512]{2,1,0:T(8,128)(2,1)} %param.7), kind=kOutput, calls=%fused_computation.12 | convolution fusion | flops 201523200 | bytes 1310720 | tf_op jit(solution)/shard_map/dot_general | solution.py:168
  14.9 2.3 %convolution_convert_fusion.7.go_ref = bf16[384,512]{1,0:T(8,128)(2,1)} fusion(bf16[512,512]{1,0:T(8,128)(2,1)} %param.13, bf16[1,384,512]{2,1,0:T(8,128)(2,1)} %param.9), kind=kOutput, calls=%fused_computation.11 | convolution fusion | flops 201523200 | bytes 1310720 | tf_op jit(solution)/shard_map/dot_general | solution.py:169
  17.3 3.5 %collective-permute-done = bf16[384,512]{1,0:T(8,128)(2,1)S(1)} collective-permute-done((bf16[384,512]{1,0:T(8,128)(2,1)}, bf16[384,512]{1,0:T(8,128)(2,1)S(1)}, u32[]{:S(2)}, u32[]{:S(2)}) %collective-permute-start) | collective-permute-done | bytes 393248 | tf_op jit(solution)/shard_map/ppermute | solution.py:26
  21.6 1.1 collective-permute-done.1
  23.4 10.9 %collective-permute-done.2 = bf16[384,512]{1,0:T(8,128)(2,1)S(1)} collective-permute-done((bf16[384,512]{1,0:T(8,128)(2,1)}, bf16[384,512]{1,0:T(8,128)(2,1)S(1)}, u32[]{:S(2)}, u32[]{:S(2)}) %collective-permute-start.2) | collective-permute-done | bytes 393248 | tf_op jit(solution)/shard_map/ppermute | solution.py:21
  36.7 4.6 %convolution_convert_fusion.v_ref = bf16[2304,512]{1,0:T(8,128)(2,1)} fusion(bf16[2304,512]{1,0:T(8,128)(2,1)} %constant_dynamic-update-slice_fusion, bf16[512,512]{1,0:T(8,128)(2,1)S(1)} %copy-done), kind=kOutput, calls=%fused_computation.1 | convolution fusion | flops 1209139200 | bytes 5242880 | tf_op jit(solution)/shard_map/dot_general | solution.py:177
  41.3 2.9 %convolution_convert_fusion.1.k_ref = bf16[2304,512]{1,0:T(8,128)(2,1)} fusion(bf16[2304,512]{1,0:T(8,128)(2,1)S(1)} %copy-done.13, bf16[512,512]{1,0:T(8,128)(2,1)S(1)} %copy-done.12), kind=kOutput, calls=%fused_computation.2 | convolution fusion | flops 1209139200 | bytes 5242880 | tf_op jit(solution)/shard_map/dot_general | solution.py:176
  44.1 0.9 broadcast_in_dim.30
  45.0 31.6 %attention.1 = (bf16[384,512]{1,0:T(8,128)(2,1)}, bf16[384,512]{1,0:T(8,128)(2,1)}, bf16[512,2304]{1,0:T(8,128)(2,1)}, bf16[512,2304]{1,0:T(8,128)(2,1)}) custom-call(bf16[384,512]{1,0:T(8,128)(2,1)} %convolution_convert_fusion.8.q_ref, bf16[2304,512]{1,0:T(8,128)(2,1)} %convolution_convert_fusion.1.k_ref, bf16[2304,512]{1,0:T(8,128)(2,1)} %convolution_convert_fusion.v_ref, ...), custom_call_target="tpu_custom_call" | custom-call | tf_op jit(solution)/shard_map/attention/pallas_call | solution.py:93
  76.6 3.2 %convolution_convert_fusion.4 = bf16[512,512]{1,0:T(8,128)(2,1)S(1)} fusion(bf16[2304,512]{1,0:T(8,128)(2,1)S(1)} %copy-done.13, bf16[512,2304]{1,0:T(8,128)(2,1)} %get-tuple-element.12), kind=kOutput, calls=%fused_computation.8 | convolution fusion | flops 1208221696 | bytes 5242880 | tf_op jit(solution)/shard_map/dot_general | solution.py:192
  79.9 1.4 convolution_convert_fusion.5
  82.5 1.0 constant_dynamic-slice_fusion.6
  83.6 3.0 %collective-permute-done.10 = bf16[1024,512]{1,0:T(8,128)(2,1)} collective-permute-done((bf16[1024,512]{1,0:T(8,128)(2,1)}, bf16[1024,512]{1,0:T(8,128)(2,1)}, u32[]{:S(2)}, u32[]{:S(2)}) %collective-permute-start.10) | collective-permute-done | bytes 1048608 | tf_op jit(solution)/shard_map/ppermute | solution.py:21
  86.6 1.5 add_convert_fusion
  88.1 1.0 copy-done.2
  89.0 0.9 constant_dynamic-slice_fusion.5
  90.7 2.8 %collective-permute-start.13 = (bf16[256,512]{1,0:T(8,128)(2,1)}, bf16[256,512]{1,0:T(8,128)(2,1)}, u32[]{:S(2)}, u32[]{:S(2)}) collective-permute-start(bf16[256,512]{1,0:T(8,128)(2,1)} %get-tuple-element.26), channel_id=1, source_target_pairs={{0,3},{1,2},{2,1},{3,0},{4,7},{5,6},{6,5},{7,4},{8,11},{9,10},{10,... | collective-permute-start | bytes 786440 | tf_op jit(solution)/shard_map/ppermute | solution.py:21
  93.4 5.9 %collective-permute-done.11 = bf16[256,512]{1,0:T(8,128)(2,1)S(1)} collective-permute-done((bf16[256,512]{1,0:T(8,128)(2,1)}, bf16[256,512]{1,0:T(8,128)(2,1)S(1)}, u32[]{:S(2)}, u32[]{:S(2)}) %collective-permute-start.11) | collective-permute-done | bytes 262176 | tf_op jit(solution)/shard_map/ppermute | solution.py:21
  99.3 4.9 %collective-permute-done.12 = bf16[256,512]{1,0:T(8,128)(2,1)} collective-permute-done((bf16[256,512]{1,0:T(8,128)(2,1)}, bf16[256,512]{1,0:T(8,128)(2,1)}, u32[]{:S(2)}, u32[]{:S(2)}) %collective-permute-start.12) | collective-permute-done | bytes 262176 | tf_op jit(solution)/shard_map/ppermute | solution.py:21
  104.2 1.2 add_convert_fusion.2
  106.2 3.1 %collective-permute-start.15 = (bf16[64,512]{1,0:T(8,128)(2,1)S(1)}, bf16[64,512]{1,0:T(8,128)(2,1)S(1)}, u32[]{:S(2)}, u32[]{:S(2)}) collective-permute-start(bf16[64,512]{1,0:T(8,128)(2,1)S(1)} %get-tuple-element.30), channel_id=1, source_target_pairs={{0,8},{1,9},{2,10},{3,11},{4,12},{5,13},{6,14},{7,15},{8,0},{9,1},... | collective-permute-start | bytes 196616 | tf_op jit(solution)/shard_map/ppermute | solution.py:21
  110.0 2.6 %fusion.12 = f32[2304,512]{1,0:T(8,128)S(1)} fusion(bf16[512,2304]{1,0:T(8,128)(2,1)S(1)} %copy-done.5, bf16[512,512]{1,0:T(8,128)(2,1)} %param.11), kind=kOutput, calls=%fused_computation.54 | convolution fusion | flops 1207959552 | bytes 7602176 | tf_op jit(solution)/shard_map/dot_general | solution.py:180
  112.6 0.8 collective-permute-done.15
  113.4 2.0 %collective-permute-done.16 = bf16[64,512]{1,0:T(8,128)(2,1)S(1)} collective-permute-done((bf16[64,512]{1,0:T(8,128)(2,1)S(1)}, bf16[64,512]{1,0:T(8,128)(2,1)S(1)}, u32[]{:S(2)}, u32[]{:S(2)}) %collective-permute-start.16) | collective-permute-done | bytes 65568 | tf_op jit(solution)/shard_map/ppermute | solution.py:21
  115.6 1.4 fusion.11
  117.0 1.7 %collective-permute-start.18 = (bf16[64,512]{1,0:T(8,128)(2,1)S(1)}, bf16[64,512]{1,0:T(8,128)(2,1)S(1)}, u32[]{:S(2)}, u32[]{:S(2)}) collective-permute-start(bf16[64,512]{1,0:T(8,128)(2,1)S(1)} %get-tuple-element.15), channel_id=1, source_target_pairs={{0,8},{1,9},{2,10},{3,11},{4,12},{5,13},{6,14},{7,15},{8,0},{9,1},... | collective-permute-start | bytes 196616 | tf_op jit(solution)/shard_map/ppermute | solution.py:21
  118.8 2.7 %collective-permute-start.19 = (bf16[64,512]{1,0:T(8,128)(2,1)S(1)}, bf16[64,512]{1,0:T(8,128)(2,1)S(1)}, u32[]{:S(2)}, u32[]{:S(2)}) collective-permute-start(bf16[64,512]{1,0:T(8,128)(2,1)S(1)} %get-tuple-element.15), channel_id=1, source_target_pairs={{0,12},{1,13},{2,14},{3,15},{4,8},{5,9},{6,10},{7,11},{8,4},{9,5},... | collective-permute-start | bytes 196616 | tf_op jit(solution)/shard_map/ppermute | solution.py:21
  122.3 2.6 %collective-permute-done.19 = bf16[64,512]{1,0:T(8,128)(2,1)S(1)} collective-permute-done((bf16[64,512]{1,0:T(8,128)(2,1)S(1)}, bf16[64,512]{1,0:T(8,128)(2,1)S(1)}, u32[]{:S(2)}, u32[]{:S(2)}) %collective-permute-start.19) | collective-permute-done | bytes 65568 | tf_op jit(solution)/shard_map/ppermute | solution.py:21
  124.8 1.5 collective-permute-start.20
  127.5 1.4 collective-permute-start.22
  129.0 3.3 %collective-permute-done.20 = bf16[256,512]{1,0:T(8,128)(2,1)S(1)} collective-permute-done((bf16[256,512]{1,0:T(8,128)(2,1)S(1)}, bf16[256,512]{1,0:T(8,128)(2,1)S(1)}, u32[]{:S(2)}, u32[]{:S(2)}) %collective-permute-start.20) | collective-permute-done | bytes 262176 | tf_op jit(solution)/shard_map/ppermute | solution.py:21
  132.4 4.0 %collective-permute-done.21 = bf16[256,512]{1,0:T(8,128)(2,1)S(1)} collective-permute-done((bf16[256,512]{1,0:T(8,128)(2,1)S(1)}, bf16[256,512]{1,0:T(8,128)(2,1)S(1)}, u32[]{:S(2)}, u32[]{:S(2)}) %collective-permute-start.21) | collective-permute-done | bytes 262176 | tf_op jit(solution)/shard_map/ppermute | solution.py:21
  136.6 1.3 collective-permute-start.6
  137.9 1.8 %collective-permute-start.7 = (bf16[384,512]{1,0:T(8,128)(2,1)S(1)}, bf16[384,512]{1,0:T(8,128)(2,1)S(1)}, u32[]{:S(2)}, u32[]{:S(2)}) collective-permute-start(bf16[384,512]{1,0:T(8,128)(2,1)S(1)} %get-tuple-element.19), channel_id=1, source_target_pairs={{0,2},{1,3},{2,0},{3,1},{4,6},{5,7},{6,4},{7,5},{8,10},{9,11},{10,... | collective-permute-start | bytes 1179656 | tf_op jit(solution)/shard_map/ppermute | solution.py:21
  139.7 2.0 %collective-permute-start.8 = (bf16[384,512]{1,0:T(8,128)(2,1)S(1)}, bf16[384,512]{1,0:T(8,128)(2,1)S(1)}, u32[]{:S(2)}, u32[]{:S(2)}) collective-permute-start(bf16[384,512]{1,0:T(8,128)(2,1)S(1)} %get-tuple-element.18), channel_id=1, source_target_pairs={{0,15},{1,0},{2,1},{3,2},{4,3},{5,4},{6,5},{7,6},{8,7},{9,8},{10,9... | collective-permute-start | bytes 1179656 | tf_op jit(solution)/shard_map/ppermute | solution.py:26
  141.7 1.8 %collective-permute-done.5 = bf16[384,512]{1,0:T(8,128)(2,1)S(1)} collective-permute-done((bf16[384,512]{1,0:T(8,128)(2,1)S(1)}, bf16[384,512]{1,0:T(8,128)(2,1)S(1)}, u32[]{:S(2)}, u32[]{:S(2)}) %collective-permute-start.5) | collective-permute-done | bytes 393248 | tf_op jit(solution)/shard_map/ppermute | solution.py:21
  143.5 0.9 collective-permute-start.9
  144.4 1.1 fusion.1
  145.5 5.8 %collective-permute-done.6 = bf16[384,512]{1,0:T(8,128)(2,1)S(1)} collective-permute-done((bf16[384,512]{1,0:T(8,128)(2,1)S(1)}, bf16[384,512]{1,0:T(8,128)(2,1)S(1)}, u32[]{:S(2)}, u32[]{:S(2)}) %collective-permute-start.6) | collective-permute-done | bytes 393248 | tf_op jit(solution)/shard_map/ppermute | solution.py:21
  151.4 3.9 %collective-permute-done.8 = bf16[384,512]{1,0:T(8,128)(2,1)S(1)} collective-permute-done((bf16[384,512]{1,0:T(8,128)(2,1)S(1)}, bf16[384,512]{1,0:T(8,128)(2,1)S(1)}, u32[]{:S(2)}, u32[]{:S(2)}) %collective-permute-start.8) | collective-permute-done | bytes 393248 | tf_op jit(solution)/shard_map/ppermute | solution.py:26
  155.3 4.8 %collective-permute-done.9 = bf16[384,512]{1,0:T(8,128)(2,1)S(1)} collective-permute-done((bf16[384,512]{1,0:T(8,128)(2,1)S(1)}, bf16[384,512]{1,0:T(8,128)(2,1)S(1)}, u32[]{:S(2)}, u32[]{:S(2)}) %collective-permute-start.9) | collective-permute-done | bytes 393248 | tf_op jit(solution)/shard_map/ppermute | solution.py:26
  160.0 1.3 fusion.2
  161.8 2.2 %fusion.10 = (f32[512,512]{1,0:T(8,128)}, f32[512,512]{1,0:T(8,128)}, f32[512,512]{1,0:T(8,128)}, f32[512,512]{1,0:T(8,128)}) fusion(bf16[2048,512]{1,0:T(8,128)(2,1)S(1)} %constant_dynamic-update-slice_fusion.6), kind=kLoop, calls=%fused_computation.52 | loop fusion | bytes 8388608 | tf_op jit(solution)/shard_map/split | solution.py:198
  (75 shorter events, 10.5 us)
Async XLA Ops:
  0.6 36.0 %copy-start = (bf16[512,512]{1,0:T(8,128)(2,1)S(1)}, bf16[512,512]{1,0:T(8,128)(2,1)}, u32[]{:S(2)}) copy-start(bf16[512,512]{1,0:T(8,128)(2,1)} %param.12) | copy-start | bytes 1572868
  0.6 16.5 %copy-start.14 = (s32[1,3,18]{2,0,1:T(1,128)S(1)}, s32[1,3,18]{2,0,1:T(1,128)}, u32[]{:S(2)}) copy-start(s32[1,3,18]{2,0,1:T(1,128)} %param.8) | copy-start | bytes 652
  0.7 20.1 %collective-permute-start = (bf16[384,512]{1,0:T(8,128)(2,1)}, bf16[384,512]{1,0:T(8,128)(2,1)S(1)}, u32[]{:S(2)}, u32[]{:S(2)}) collective-permute-start(bf16[384,512]{1,0:T(8,128)(2,1)} %bitcast.44), channel_id=1, source_target_pairs={{0,1},{1,2},{2,3},{3,4},{4,5},{5,6},{6,7},{7,8},{8,9},{9,10},{10,1... | collective-permute-start | bytes 1179656 | tf_op jit(solution)/shard_map/ppermute | solution.py:26
  3.7 19.0 %collective-permute-start.1 = (bf16[384,512]{1,0:T(8,128)(2,1)}, bf16[384,512]{1,0:T(8,128)(2,1)S(1)}, u32[]{:S(2)}, u32[]{:S(2)}) collective-permute-start(bf16[384,512]{1,0:T(8,128)(2,1)} %bitcast.45), channel_id=1, source_target_pairs={{0,15},{1,0},{2,1},{3,2},{4,3},{5,4},{6,5},{7,6},{8,7},{9,8},{10,9... | collective-permute-start | bytes 1179656 | tf_op jit(solution)/shard_map/ppermute | solution.py:26
  7.7 26.6 %collective-permute-start.2 = (bf16[384,512]{1,0:T(8,128)(2,1)}, bf16[384,512]{1,0:T(8,128)(2,1)S(1)}, u32[]{:S(2)}, u32[]{:S(2)}) collective-permute-start(bf16[384,512]{1,0:T(8,128)(2,1)} %bitcast.46), channel_id=1, source_target_pairs={{0,8},{1,9},{2,10},{3,11},{4,12},{5,13},{6,14},{7,15},{8,0},{9,1},... | collective-permute-start | bytes 1179656 | tf_op jit(solution)/shard_map/ppermute | solution.py:21
  8.6 26.5 %collective-permute-start.3 = (bf16[384,512]{1,0:T(8,128)(2,1)}, bf16[384,512]{1,0:T(8,128)(2,1)S(1)}, u32[]{:S(2)}, u32[]{:S(2)}) collective-permute-start(bf16[384,512]{1,0:T(8,128)(2,1)} %bitcast.47), channel_id=1, source_target_pairs={{0,4},{1,5},{2,6},{3,7},{4,0},{5,1},{6,2},{7,3},{8,12},{9,13},{10,... | collective-permute-start | bytes 1179656 | tf_op jit(solution)/shard_map/ppermute | solution.py:21
  10.2 25.7 %collective-permute-start.4 = (bf16[384,512]{1,0:T(8,128)(2,1)}, bf16[384,512]{1,0:T(8,128)(2,1)S(1)}, u32[]{:S(2)}, u32[]{:S(2)}) collective-permute-start(bf16[384,512]{1,0:T(8,128)(2,1)} %bitcast.48), channel_id=1, source_target_pairs={{0,2},{1,3},{2,0},{3,1},{4,6},{5,7},{6,4},{7,5},{8,10},{9,11},{10,... | collective-permute-start | bytes 1179656 | tf_op jit(solution)/shard_map/ppermute | solution.py:21
  36.7 4.6 %copy-start.12 = (bf16[512,512]{1,0:T(8,128)(2,1)S(1)}, bf16[512,512]{1,0:T(8,128)(2,1)}, u32[]{:S(2)}) copy-start(bf16[512,512]{1,0:T(8,128)(2,1)} %param.11) | copy-start | bytes 1572868
  36.7 4.6 %copy-start.13 = (bf16[2304,512]{1,0:T(8,128)(2,1)S(1)}, bf16[2304,512]{1,0:T(8,128)(2,1)}, u32[]{:S(2)}) copy-start(bf16[2304,512]{1,0:T(8,128)(2,1)} %constant_dynamic-update-slice_fusion) | copy-start | bytes 7077892
  76.6 3.3 %copy-start.4 = (bf16[512,2304]{1,0:T(8,128)(2,1)S(1)}, bf16[512,2304]{1,0:T(8,128)(2,1)}, u32[]{:S(2)}) copy-start(bf16[512,2304]{1,0:T(8,128)(2,1)} %get-tuple-element.11) | copy-start | bytes 7077892
  79.9 1.5 copy-start.8
  79.9 1.5 copy-start.9
  79.9 1.9 %copy-start.3 = (bf16[1,384,512]{2,1,0:T(8,128)(2,1)S(1)}, bf16[1,384,512]{2,1,0:T(8,128)(2,1)}, u32[]{:S(2)}) copy-start(bf16[1,384,512]{2,1,0:T(8,128)(2,1)} %param.7) | copy-start | bytes 1179652
  79.9 1.9 %copy-start.10 = (bf16[384,512]{1,0:T(8,128)(2,1)S(1)}, bf16[384,512]{1,0:T(8,128)(2,1)}, u32[]{:S(2)}) copy-start(bf16[384,512]{1,0:T(8,128)(2,1)} %get-tuple-element.13) | copy-start | bytes 1179652
  83.5 3.0 %collective-permute-start.10 = (bf16[1024,512]{1,0:T(8,128)(2,1)}, bf16[1024,512]{1,0:T(8,128)(2,1)}, u32[]{:S(2)}, u32[]{:S(2)}) collective-permute-start(bf16[1024,512]{1,0:T(8,128)(2,1)} %constant_dynamic-slice_fusion.6), channel_id=1, source_target_pairs={{0,16},{16,0},{1,17},{17,1},{2,18},{18,2},{3,19},{19,3},{4,20},{20... | collective-permute-start | bytes 3145736 | tf_op jit(solution)/shard_map/ppermute | solution.py:21
  88.1 1.0 copy-start.2
  89.0 20.9 %copy-start.5 = (bf16[512,2304]{1,0:T(8,128)(2,1)S(1)}, bf16[512,2304]{1,0:T(8,128)(2,1)}, u32[]{:S(2)}) copy-start(bf16[512,2304]{1,0:T(8,128)(2,1)} %get-tuple-element.11) | copy-start | bytes 7077892
  89.9 9.4 %collective-permute-start.11 = (bf16[256,512]{1,0:T(8,128)(2,1)}, bf16[256,512]{1,0:T(8,128)(2,1)S(1)}, u32[]{:S(2)}, u32[]{:S(2)}) collective-permute-start(bf16[256,512]{1,0:T(8,128)(2,1)} %get-tuple-element.25), channel_id=1, source_target_pairs={{0,1},{1,0},{2,3},{3,2},{4,5},{5,4},{6,7},{7,6},{8,9},{9,8},{10,11... | collective-permute-start | bytes 786440 | tf_op jit(solution)/shard_map/ppermute | solution.py:21
  89.9 14.3 %collective-permute-start.12 = (bf16[256,512]{1,0:T(8,128)(2,1)}, bf16[256,512]{1,0:T(8,128)(2,1)}, u32[]{:S(2)}, u32[]{:S(2)}) collective-permute-start(bf16[256,512]{1,0:T(8,128)(2,1)} %get-tuple-element.27), channel_id=1, source_target_pairs={{0,2},{1,3},{2,0},{3,1},{4,6},{5,7},{6,4},{7,5},{8,10},{9,11},{10,... | collective-permute-start | bytes 786440 | tf_op jit(solution)/shard_map/ppermute | solution.py:21
  90.7 13.6 %collective-permute-start.13 = (bf16[256,512]{1,0:T(8,128)(2,1)}, bf16[256,512]{1,0:T(8,128)(2,1)}, u32[]{:S(2)}, u32[]{:S(2)}) collective-permute-start(bf16[256,512]{1,0:T(8,128)(2,1)} %get-tuple-element.26), channel_id=1, source_target_pairs={{0,3},{1,2},{2,1},{3,0},{4,7},{5,6},{6,5},{7,4},{8,11},{9,10},{10,... | collective-permute-start | bytes 786440 | tf_op jit(solution)/shard_map/ppermute | solution.py:21
  105.5 7.1 %collective-permute-start.14 = (bf16[64,512]{1,0:T(8,128)(2,1)S(1)}, bf16[64,512]{1,0:T(8,128)(2,1)S(1)}, u32[]{:S(2)}, u32[]{:S(2)}) collective-permute-start(bf16[64,512]{1,0:T(8,128)(2,1)S(1)} %get-tuple-element.28), channel_id=1, source_target_pairs={{0,4},{1,5},{2,6},{3,7},{4,0},{5,1},{6,2},{7,3},{8,12},{9,13},{10,... | collective-permute-start | bytes 196616 | tf_op jit(solution)/shard_map/ppermute | solution.py:21
  106.2 7.2 %collective-permute-start.15 = (bf16[64,512]{1,0:T(8,128)(2,1)S(1)}, bf16[64,512]{1,0:T(8,128)(2,1)S(1)}, u32[]{:S(2)}, u32[]{:S(2)}) collective-permute-start(bf16[64,512]{1,0:T(8,128)(2,1)S(1)} %get-tuple-element.30), channel_id=1, source_target_pairs={{0,8},{1,9},{2,10},{3,11},{4,12},{5,13},{6,14},{7,15},{8,0},{9,1},... | collective-permute-start | bytes 196616 | tf_op jit(solution)/shard_map/ppermute | solution.py:21
  109.3 6.1 %collective-permute-start.16 = (bf16[64,512]{1,0:T(8,128)(2,1)S(1)}, bf16[64,512]{1,0:T(8,128)(2,1)S(1)}, u32[]{:S(2)}, u32[]{:S(2)}) collective-permute-start(bf16[64,512]{1,0:T(8,128)(2,1)S(1)} %get-tuple-element.29), channel_id=1, source_target_pairs={{0,12},{1,13},{2,14},{3,15},{4,8},{5,9},{6,10},{7,11},{8,4},{9,5},... | collective-permute-start | bytes 196616 | tf_op jit(solution)/shard_map/ppermute | solution.py:21
  110.0 5.6 %copy-start.1 = (bf16[512,2304]{1,0:T(8,128)(2,1)S(1)}, bf16[512,2304]{1,0:T(8,128)(2,1)}, u32[]{:S(2)}) copy-start(bf16[512,2304]{1,0:T(8,128)(2,1)} %get-tuple-element.12) | copy-start | bytes 7077892
  115.5 6.0 %collective-permute-start.17 = (bf16[64,512]{1,0:T(8,128)(2,1)S(1)}, bf16[64,512]{1,0:T(8,128)(2,1)S(1)}, u32[]{:S(2)}, u32[]{:S(2)}) collective-permute-start(bf16[64,512]{1,0:T(8,128)(2,1)S(1)} %get-tuple-element.15), channel_id=1, source_target_pairs={{0,4},{1,5},{2,6},{3,7},{4,0},{5,1},{6,2},{7,3},{8,12},{9,13},{10,... | collective-permute-start | bytes 196616 | tf_op jit(solution)/shard_map/ppermute | solution.py:21
  117.0 5.2 %collective-permute-start.18 = (bf16[64,512]{1,0:T(8,128)(2,1)S(1)}, bf16[64,512]{1,0:T(8,128)(2,1)S(1)}, u32[]{:S(2)}, u32[]{:S(2)}) collective-permute-start(bf16[64,512]{1,0:T(8,128)(2,1)S(1)} %get-tuple-element.15), channel_id=1, source_target_pairs={{0,8},{1,9},{2,10},{3,11},{4,12},{5,13},{6,14},{7,15},{8,0},{9,1},... | collective-permute-start | bytes 196616 | tf_op jit(solution)/shard_map/ppermute | solution.py:21
  118.8 6.1 %collective-permute-start.19 = (bf16[64,512]{1,0:T(8,128)(2,1)S(1)}, bf16[64,512]{1,0:T(8,128)(2,1)S(1)}, u32[]{:S(2)}, u32[]{:S(2)}) collective-permute-start(bf16[64,512]{1,0:T(8,128)(2,1)S(1)} %get-tuple-element.15), channel_id=1, source_target_pairs={{0,12},{1,13},{2,14},{3,15},{4,8},{5,9},{6,10},{7,11},{8,4},{9,5},... | collective-permute-start | bytes 196616 | tf_op jit(solution)/shard_map/ppermute | solution.py:21
  124.8 7.5 %collective-permute-start.20 = (bf16[256,512]{1,0:T(8,128)(2,1)S(1)}, bf16[256,512]{1,0:T(8,128)(2,1)S(1)}, u32[]{:S(2)}, u32[]{:S(2)}) collective-permute-start(bf16[256,512]{1,0:T(8,128)(2,1)S(1)} %constant_dynamic-update-slice_fusion.12), channel_id=1, source_target_pairs={{0,1},{1,0},{2,3},{3,2},{4,5},{5,4},{6,7},{7,6},{8,9},{9,8},{10,11... | collective-permute-start | bytes 786440 | tf_op jit(solution)/shard_map/ppermute | solution.py:21
  126.4 10.1 %collective-permute-start.21 = (bf16[256,512]{1,0:T(8,128)(2,1)S(1)}, bf16[256,512]{1,0:T(8,128)(2,1)S(1)}, u32[]{:S(2)}, u32[]{:S(2)}) collective-permute-start(bf16[256,512]{1,0:T(8,128)(2,1)S(1)} %constant_dynamic-update-slice_fusion.12), channel_id=1, source_target_pairs={{0,2},{1,3},{2,0},{3,1},{4,6},{5,7},{6,4},{7,5},{8,10},{9,11},{10,... | collective-permute-start | bytes 786440 | tf_op jit(solution)/shard_map/ppermute | solution.py:21
  127.1 17.3 %copy-start.6 = (bf16[512,512]{1,0:T(8,128)(2,1)S(1)}, bf16[512,512]{1,0:T(8,128)(2,1)}, u32[]{:S(2)}) copy-start(bf16[512,512]{1,0:T(8,128)(2,1)} %param.13) | copy-start | bytes 1572868
  127.1 32.9 %copy-start.7 = (bf16[512,512]{1,0:T(8,128)(2,1)S(1)}, bf16[512,512]{1,0:T(8,128)(2,1)}, u32[]{:S(2)}) copy-start(bf16[512,512]{1,0:T(8,128)(2,1)} %param.10) | copy-start | bytes 1572868
  127.1 32.9 %copy-start.11 = (bf16[384,512]{1,0:T(8,128)(2,1)S(1)}, bf16[384,512]{1,0:T(8,128)(2,1)}, u32[]{:S(2)}) copy-start(bf16[384,512]{1,0:T(8,128)(2,1)} %get-tuple-element.13) | copy-start | bytes 1179652
  127.1 16.3 %collective-permute-start.5 = (bf16[384,512]{1,0:T(8,128)(2,1)S(1)}, bf16[384,512]{1,0:T(8,128)(2,1)S(1)}, u32[]{:S(2)}, u32[]{:S(2)}) collective-permute-start(bf16[384,512]{1,0:T(8,128)(2,1)S(1)} %get-tuple-element.16), channel_id=1, source_target_pairs={{0,8},{1,9},{2,10},{3,11},{4,12},{5,13},{6,14},{7,15},{8,0},{9,1},... | collective-permute-start | bytes 1179656 | tf_op jit(solution)/shard_map/ppermute | solution.py:21
  127.5 9.0 %collective-permute-start.22 = (bf16[256,512]{1,0:T(8,128)(2,1)S(1)}, bf16[256,512]{1,0:T(8,128)(2,1)S(1)}, u32[]{:S(2)}, u32[]{:S(2)}) collective-permute-start(bf16[256,512]{1,0:T(8,128)(2,1)S(1)} %constant_dynamic-update-slice_fusion.12), channel_id=1, source_target_pairs={{0,3},{1,2},{2,1},{3,0},{4,7},{5,6},{6,5},{7,4},{8,11},{9,10},{10,... | collective-permute-start | bytes 786440 | tf_op jit(solution)/shard_map/ppermute | solution.py:21
  136.5 25.1 %collective-permute-start.23 = (bf16[1024,512]{1,0:T(8,128)(2,1)S(1)}, bf16[1024,512]{1,0:T(8,128)(2,1)S(1)}, u32[]{:S(2)}, u32[]{:S(2)}) collective-permute-start(bf16[1024,512]{1,0:T(8,128)(2,1)S(1)} %constant_dynamic-update-slice_fusion.8), channel_id=1, source_target_pairs={{0,16},{16,0},{1,17},{17,1},{2,18},{18,2},{3,19},{19,3},{4,20},{20... | collective-permute-start | bytes 3145736 | tf_op jit(solution)/shard_map/ppermute | solution.py:21
  136.6 14.8 %collective-permute-start.6 = (bf16[384,512]{1,0:T(8,128)(2,1)S(1)}, bf16[384,512]{1,0:T(8,128)(2,1)S(1)}, u32[]{:S(2)}, u32[]{:S(2)}) collective-permute-start(bf16[384,512]{1,0:T(8,128)(2,1)S(1)} %get-tuple-element.20), channel_id=1, source_target_pairs={{0,4},{1,5},{2,6},{3,7},{4,0},{5,1},{6,2},{7,3},{8,12},{9,13},{10,... | collective-permute-start | bytes 1179656 | tf_op jit(solution)/shard_map/ppermute | solution.py:21
  137.9 13.5 %collective-permute-start.7 = (bf16[384,512]{1,0:T(8,128)(2,1)S(1)}, bf16[384,512]{1,0:T(8,128)(2,1)S(1)}, u32[]{:S(2)}, u32[]{:S(2)}) collective-permute-start(bf16[384,512]{1,0:T(8,128)(2,1)S(1)} %get-tuple-element.19), channel_id=1, source_target_pairs={{0,2},{1,3},{2,0},{3,1},{4,6},{5,7},{6,4},{7,5},{8,10},{9,11},{10,... | collective-permute-start | bytes 1179656 | tf_op jit(solution)/shard_map/ppermute | solution.py:21
  139.7 15.6 %collective-permute-start.8 = (bf16[384,512]{1,0:T(8,128)(2,1)S(1)}, bf16[384,512]{1,0:T(8,128)(2,1)S(1)}, u32[]{:S(2)}, u32[]{:S(2)}) collective-permute-start(bf16[384,512]{1,0:T(8,128)(2,1)S(1)} %get-tuple-element.18), channel_id=1, source_target_pairs={{0,15},{1,0},{2,1},{3,2},{4,3},{5,4},{6,5},{7,6},{8,7},{9,8},{10,9... | collective-permute-start | bytes 1179656 | tf_op jit(solution)/shard_map/ppermute | solution.py:26
  143.5 16.5 %collective-permute-start.9 = (bf16[384,512]{1,0:T(8,128)(2,1)S(1)}, bf16[384,512]{1,0:T(8,128)(2,1)S(1)}, u32[]{:S(2)}, u32[]{:S(2)}) collective-permute-start(bf16[384,512]{1,0:T(8,128)(2,1)S(1)} %get-tuple-element.17), channel_id=1, source_target_pairs={{0,1},{1,2},{2,3},{3,4},{4,5},{5,6},{6,7},{7,8},{8,9},{9,10},{10,1... | collective-permute-start | bytes 1179656 | tf_op jit(solution)/shard_map/ppermute | solution.py:26
